TPU v7x, 128 devices: a whole 4x4x4 slice. The times are simulated.
128 devices in a mesh: row: 4 (over y), col: 32 (over z, x, core).
Axes of the slice: x: 4, y: 4, z: 4, core: 2. Of those that a mesh axis runs over, the one named last changes fastest.
Arguments:
- rhs: float32 [16384, 256], P(('row', 'col')), may hold values from -6 to 6
- dense: float32 [2, 16384, 16384], P(None, 'col', 'row'), may hold values from -0.03125 to 0.03125
- inflow: float32 [128, 2, 2, 512, 256], P(('row', 'col')), may hold values from -0.25 to 0.25
- robin: float32 [128, 2, 2, 512, 512], P(('row', 'col')), may hold values from -0.1875 to 0.1875
- outflow: float32 [128, 2, 256, 1024], P(('row', 'col')), may hold values from -0.0390625 to 0.0390625
- trace_row: int32 [32, 128, 8], replicated, may hold values from 0 to 511
- trace_count: int32 [32, 128], replicated, may hold values from 0 to 8, as said below
- current_row: int32 [128, 128, 2], replicated, may hold values from 0 to 127
- current_count: int32 [128, 128], replicated, may hold values from 0 to 2, as said below
Outputs:
- solution: float32 [16384, 256], P(('row', 'col'))
Inputs may be any that keep to these rules, and one draw needn't show every extreme that they name: `trace_row`: repeats may occur. `trace_count`: 8 is reached, and some subdomain takes 8 from every block. `current_row`: repeats may occur. `current_count`: some subdomain gives 2 to every block, and some block receives 2 from every subdomain.
All inputs are finite; a program needn't handle non-finite values.
Results may differ from a plain program's by a relative error of at most 0.0001.
Values sent between devices are 32-bit elements; how exact they have to be, the bound alone decides.
A program may use at most 128 MiB of HBM per device.

v0:
```python
import jax
import jax.numpy as jnp
from jax import lax
from jax.sharding import PartitionSpec as P

ITERS = 2
EPS = 1e-06
SCALE = 2.0 ** (-24)
HIGH = lax.Precision.HIGH


def extended(x, sides, width):
    for axis, dim in sides:
        size, length = (lax.axis_size(axis), x.shape[dim])
        up = [(i, (i + 1) % size) for i in range(size - 1)]
        down = [(j, i) for i, j in up]
        last = lax.slice_in_dim(x, length - width, length, axis=dim)
        leading = lax.slice_in_dim(x, 0, width, axis=dim)
        before = lax.ppermute(last, axis, up)
        after = lax.ppermute(leading, axis, down)
        x = jnp.concatenate([before, x, after], axis=dim)
    return x


def combine(real_half, imag_half, waves):
    return jnp.concatenate(
        [
            real_half[..., :waves] - imag_half[..., waves:],
            real_half[..., waves:] + imag_half[..., :waves],
        ],
        axis=-1,
    )


def scale_vector(vector, coef, waves):
    real_part = vector[:, :waves]
    imag_part = vector[:, waves:]
    return jnp.concatenate(
        [coef[0] * real_part - coef[1] * imag_part, coef[0] * imag_part + coef[1] * real_part],
        axis=1,
    )


def inner_terms(left, right, waves):
    left_real, left_imag = (left[:, :waves], left[:, waves:])
    right_real, right_imag = (right[:, :waves], right[:, waves:])
    return (
        jnp.sum(left_real * right_real + left_imag * right_imag, axis=0),
        jnp.sum(left_real * right_imag - left_imag * right_real, axis=0),
    )


def square_terms(vector, waves):
    halves = jnp.sum(vector * vector, axis=0)
    return halves[:waves] + halves[waves:]


def cmul(first, second):
    return (
        first[0] * second[0] - first[1] * second[1],
        first[0] * second[1] + first[1] * second[0],
    )


def cconj(first):
    return (first[0], -first[1])


def csub(first, second):
    return (first[0] - second[0], first[1] - second[1])


def cadd(first, second):
    return (first[0] + second[0], first[1] + second[1])


def cdiv(first, second):
    denom = second[0] * second[0] + second[1] * second[1]
    numer = cmul(first, cconj(second))
    return (numer[0] / denom, numer[1] / denom)


def solve_small(gram, target):
    size = len(target)
    gram = [list(line) for line in gram]
    target = list(target)
    for pivot in range(size):
        for lower in range(pivot + 1, size):
            factor = cdiv(gram[lower][pivot], gram[pivot][pivot])
            for other in range(pivot, size):
                gram[lower][other] = csub(gram[lower][other], cmul(factor, gram[pivot][other]))
            target[lower] = csub(target[lower], cmul(factor, target[pivot]))
    result = [None] * size
    for pivot in reversed(range(size)):
        summed = target[pivot]
        for other in range(pivot + 1, size):
            summed = csub(summed, cmul(gram[pivot][other], result[other]))
        result[pivot] = cdiv(summed, gram[pivot][pivot])
    return result


def least_squares(hess, beta, steps):
    zero_pair = (jnp.zeros_like(beta), jnp.zeros_like(beta))
    gram = []
    for first in range(steps):
        line = []
        for second in range(steps):
            summed = zero_pair
            for height in range(steps + 1):
                summed = cadd(
                    summed,
                    cmul(
                        cconj(hess.get((height, first), zero_pair)),
                        hess.get((height, second), zero_pair),
                    ),
                )
            line.append(summed)
        gram.append(line)
    target = [
        cmul(cconj(hess.get((0, first), zero_pair)), (beta, jnp.zeros_like(beta)))
        for first in range(steps)
    ]
    return solve_small(gram, target)


def turned(vector, waves):
    return jnp.concatenate([-vector[..., waves:], vector[..., :waves]], axis=-1)


def conj_mul(first, second):
    return cmul(cconj(first), second)


def krylov_coefficients(sums):
    norm0, p_real, p_imag, norm1, t_real, t_imag, s_real, s_imag, norm2 = sums
    zero = jnp.zeros_like(norm0)
    beta2 = norm0 + EPS
    beta = jnp.sqrt(beta2)
    unit = norm0 / beta2
    lack = EPS / beta2
    p = (p_real / beta2, p_imag / beta2)
    q = norm1 / beta2
    back = 1.0 / SCALE
    t = (t_real / beta2 * back, t_imag / beta2 * back)
    s = (s_real / beta2 * back, s_imag / beta2 * back)
    z = norm2 / beta2 * back * back
    p_abs = p[0] * p[0] + p[1] * p[1]
    h00 = (unit + p[0], p[1])
    h10 = jnp.sqrt(unit * lack + 2.0 * lack * p[0] + (q - p_abs) + EPS)
    a = 1.0 / h10
    g = (lack - p[0], -p[1])
    g_abs = g[0] * g[0] + g[1] * g[1]
    gp = cmul(g, p)
    h01 = (a * (lack * h00[0] + (t[0] + gp[0])), a * (lack * h00[1] + (t[1] + gp[1])))
    short = a * a * (lack * (1.0 - lack) * (unit + 2.0 * p[0]) + lack * p_abs + EPS)
    length = 1.0 - short
    gt = conj_mul(g, t)
    m = (
        a * a * (s[0] + g[0] * q + gt[0] + g_abs * p[0]),
        a * a * (s[1] + g[1] * q + gt[1] + g_abs * p[1]),
    )
    spread = a * a * (z + 2.0 * conj_mul(g, s)[0] + g_abs * q)
    h11 = (length + m[0], m[1])
    remain = length * short + 2.0 * short * m[0] + (spread - m[0] * m[0] - m[1] * m[1])
    remain = remain - h01[0] * h01[0] - h01[1] * h01[1]
    h21 = jnp.sqrt(remain + EPS)
    hess = {(0, 0): h00, (1, 0): (h10, zero), (0, 1): h01, (1, 1): h11, (2, 1): (h21, zero)}
    y0, y1 = least_squares(hess, beta, ITERS)
    ya = (y1[0] * a, y1[1] * a)
    yg = cmul(ya, g)
    return (((y0[0] + yg[0]) / beta, (y0[1] + yg[1]) / beta), (ya[0] / beta, ya[1] / beta))


def on_device(
    rhs, dense, inflow, robin, outflow, trace_row, trace_count, current_row, current_count
):
    n_row = lax.axis_size("row")
    n_col = lax.axis_size("col")
    devices = n_row * n_col
    row_at = lax.axis_index("row")
    col_at = lax.axis_index("col")
    device_at = row_at * n_col + col_at
    block_rows, lanes = rhs.shape
    waves = lanes // 2
    tpair = trace_row.shape[2]
    tback = current_row.shape[2]
    inflow_mine = inflow[0]
    robin_mine = robin[0]
    outflow_mine = outflow[0]
    trace_rows = lax.dynamic_index_in_dim(trace_row, col_at, 0, keepdims=False)
    trace_live = lax.dynamic_index_in_dim(trace_count, col_at, 0, keepdims=False)
    trace_keep = (jnp.arange(tpair, dtype=jnp.int32)[None, :] < trace_live[:, None]).astype(
        jnp.float32
    )
    basis = [rhs]
    for step in range(ITERS):
        operate_vector = basis[step] if step == 0 else basis[step] * SCALE
        piece = lax.all_gather(operate_vector, "col", axis=0, tiled=True)
        real_cols = dense[0]
        imag_cols = dense[1]
        field = jnp.dot(real_cols, piece, precision=HIGH, preferred_element_type=jnp.float32)
        field = field + jnp.dot(
            imag_cols, turned(piece, waves), precision=HIGH, preferred_element_type=jnp.float32
        )
        buffer = (
            jnp.take(field, trace_rows.reshape(-1), axis=0).reshape(devices, tpair, lanes)
            * trace_keep[:, :, None]
        )
        arrived = lax.all_to_all(buffer, ("row", "col"), split_axis=0, concat_axis=0, tiled=True)
        slots = jnp.sum(arrived.reshape(n_row, n_col, tpair, lanes), axis=0)
        slots = slots.reshape(n_col * tpair, lanes)
        mixed = jnp.einsum("fpmk,kl->fpml", inflow_mine, slots, precision=HIGH)
        excite = combine(mixed[:, 0], mixed[:, 1], waves)
        mixed = jnp.einsum("fpmn,fnl->fpml", robin_mine, excite, precision=HIGH)
        local = combine(mixed[:, 0], mixed[:, 1], waves)
        padded = extended(local, ((("row", "col"), 0),), 1)
        near = jnp.stack([padded[0], padded[3]], axis=0)
        mixed = jnp.einsum("fpmn,fnl->fpml", robin_mine, near, precision=HIGH)
        faces = local + combine(mixed[:, 0], mixed[:, 1], waves)
        flat = faces.reshape(faces.shape[0] * faces.shape[1], lanes)
        mixed = jnp.einsum("pkn,nl->pkl", outflow_mine, flat, precision=HIGH)
        currents = combine(mixed[0], mixed[1], waves)
        operate_arrived = lax.all_to_all(
            currents.reshape(devices, tback, lanes),
            ("row", "col"),
            split_axis=0,
            concat_axis=0,
            tiled=True,
        )
        own_rows = lax.dynamic_index_in_dim(current_row, device_at, 0, keepdims=False)
        own_live = lax.dynamic_index_in_dim(current_count, device_at, 0, keepdims=False)
        alive = (jnp.arange(tback, dtype=jnp.int32)[None, :] < own_live[:, None]).astype(
            jnp.float32
        )
        landed = (
            jnp.zeros((block_rows, lanes), jnp.float32)
            .at[own_rows.reshape(-1)]
            .add((operate_arrived * alive[..., None]).reshape(-1, lanes))
        )
        basis.append(landed)
    u0, b0, b1 = basis
    sums = [square_terms(u0, waves), *inner_terms(u0, b0, waves), square_terms(b0, waves)]
    sums += [*inner_terms(u0, b1, waves), *inner_terms(b0, b1, waves), square_terms(b1, waves)]
    sums = lax.psum(jnp.stack(sums, axis=0), ("row", "col"))
    first, second = krylov_coefficients([sums[i] for i in range(9)])
    return scale_vector(u0, first, waves) + scale_vector(b0, second, waves)


def solution(mesh):
    placed = (
        P(("row", "col"), None),
        P(None, "col", "row"),
        P(("row", "col"), None, None, None, None),
        P(("row", "col"), None, None, None, None),
        P(("row", "col"), None, None, None),
        P(),
        P(),
        P(),
        P(),
    )
    return jax.shard_map(
        on_device, mesh=mesh, in_specs=placed, out_specs=P(("row", "col"), None), check_vma=False
    )
```

profile of v0, /device:TPU:1, one launch (start us, length us, event | category | flops | bytes accessed | tf_op | source)
XLA Modules:
  0.0 399.5 jit_solution(4154344122775271763)
XLA Ops:
  9.0 50.4 %all-gather.3.cloned.1.call-done = f32[4096,256]{1,0:T(8,128)} async-done(((f32[128,256]{1,0:T(8,128)}), f32[4096,256]{1,0:T(8,128)}) %all-gather.3.cloned.1.call-update) | async-done | bytes 4194320 | tf_op jit(solution)/shard_map/all_gather | solution.py:198
  62.0 7.8 %fusion.6 = f32[512,256]{1,0:T(8,128)S(1)} fusion(f32[4096,256]{1,0:T(8,128)} %all-gather.3.cloned.1.call-done, f32[2,512,4096]{2,1,0:T(8,128)} %param.12), kind=kOutput, calls=%fused_computation.10 | convolution fusion | flops 3221225472 | bytes 13107200 | tf_op jit(solution)/shard_map/dot_general | solution.py:201
  70.1 3.6 fusion.63
  73.7 4.7 %gather_fusion = f32[1024,256]{1,0:T(8,128)} fusion(f32[512,256]{1,0:T(8,128)S(1)} %fusion.63, s32[1024]{0:T(1024)S(1)} %fusion.110), kind=kCustom, calls=%fused_computation.clone | custom fusion | bytes 2101248 | tf_op jit(solution)/shard_map/jit(_take)/gather | solution.py:206
  79.9 26.8 %all_to_all.20 = f32[128,8,256]{2,1,0:T(8,128)S(1)} all-to-all(f32[128,8,256]{2,1,0:T(8,128)S(1)} %bitcast_multiply_fusion.1), channel_id=1, replica_groups=mesh['row'=4,'col'=32] {'row','col'}, dimensions={0} | all-to-all | bytes 2097152 | tf_op jit(solution)/shard_map/all_to_all | solution.py:209
  114.5 3.0 collective-permute-start
  124.0 4.4 %collective-permute-done.1 = f32[1,512,256]{1,2,0:T(8,128)} collective-permute-done((f32[1,512,256]{1,2,0:T(8,128)}, f32[1,512,256]{1,2,0:T(8,128)}, u32[]{:S(2)}, u32[]{:S(2)}) %collective-permute-start.1) | collective-permute-done | bytes 524320 | tf_op jit(solution)/shard_map/ppermute | solution.py:20
  128.4 4.4 %fusion.37 = f32[2,2,512,256]{2,3,1,0:T(8,128)S(1)} fusion(f32[1,2,2,512,512]{4,3,2,1,0:T(8,128)} %param.14, f32[1,512,256]{1,2,0:T(8,128)} %collective-permute-done.1, f32[1,512,256]{1,2,0:T(8,128)} %collective-permute-done), kind=kOutput, calls=%fused_computation.41 | convolution fusion | flops 1610874880 | bytes 7340032 | tf_op jit(solution)/shard_map/fpmn,fnl->fpml/dot_general | solution.py:218
  138.3 3.8 fusion.52
  143.2 11.1 %all-to-all-start.1 = ((f32[128,2,256]{2,1,0:T(2,128)}), f32[128,2,256]{2,1,0:T(2,128)S(1)}, u32[]{:S(2)}, u32[]{:S(2)}) async-start(f32[128,2,256]{2,1,0:T(2,128)} %reshape.140), calls=%async_computation.1 | async-start | bytes 524288 | tf_op jit(solution)/shard_map/all_to_all | solution.py:223
  155.3 10.0 %all-to-all-done.1 = f32[128,2,256]{2,1,0:T(2,128)S(1)} async-done(((f32[128,2,256]{2,1,0:T(2,128)}), f32[128,2,256]{2,1,0:T(2,128)S(1)}, u32[]{:S(2)}, u32[]{:S(2)}) %all-to-all-start.1) | async-done | bytes 262176 | tf_op jit(solution)/shard_map/all_to_all | solution.py:223
  168.4 42.9 %all-gather.5.cloned.1.call-done = f32[4096,256]{1,0:T(8,128)} async-done(((f32[128,256]{1,0:T(8,128)}), f32[4096,256]{1,0:T(8,128)}) %all-gather.5.cloned.1.call-update) | async-done | bytes 4194320 | tf_op jit(solution)/shard_map/all_gather | solution.py:198
  211.3 11.5 %fusion.4 = f32[256,512]{1,0:T(8,128)S(1)} fusion(f32[4096,256]{1,0:T(8,128)} %all-gather.5.cloned.1.call-done, f32[2,512,4096]{2,1,0:T(8,128)} %param.12), kind=kOutput, calls=%fused_computation.8 | convolution fusion | flops 3221225472 | bytes 13107200 | tf_op jit(solution)/shard_map/dot_general | solution.py:201
  223.1 9.6 %fusion.73 = f32[512,256]{0,1:T(8,128)S(1)} fusion(f32[256,512]{1,0:T(8,128)S(1)} %fusion.4, f32[2,512,4096]{2,1,0:T(8,128)} %param.12, f32[4096,128]{1,0:T(8,128)S(1)} %get-tuple-element.44, f32[4096,128]{1,0:T(8,128)S(1)} %get-tuple-element.43), kind=kOutput, calls=%fused_computation.51 | convolution fusion | flops 3222405120 | bytes 13631488 | tf_op jit(solution)/shard_map/dot_general | solution.py:202
  232.8 4.7 %gather_fusion.1 = f32[1024,256]{1,0:T(8,128)} fusion(f32[512,256]{1,0:T(8,128)S(1)} %copy.33, s32[1024]{0:T(1024)S(1)} %fusion.110), kind=kCustom, calls=%fused_computation.1.clone | custom fusion | bytes 2101248 | tf_op jit(solution)/shard_map/jit(_take)/gather | solution.py:206
  239.1 26.5 %all_to_all.21 = f32[128,8,256]{2,1,0:T(8,128)S(1)} all-to-all(f32[128,8,256]{2,1,0:T(8,128)S(1)} %bitcast_multiply_fusion), channel_id=1, replica_groups=mesh['row'=4,'col'=32] {'row','col'}, dimensions={0} | all-to-all | bytes 2097152 | tf_op jit(solution)/shard_map/all_to_all | solution.py:209
  275.0 3.0 collective-permute-start.2
  281.4 3.1 collective-permute-done.2
  284.4 4.4 %collective-permute-done.3 = f32[1,512,256]{1,2,0:T(8,128)} collective-permute-done((f32[1,512,256]{1,2,0:T(8,128)}, f32[1,512,256]{1,2,0:T(8,128)}, u32[]{:S(2)}, u32[]{:S(2)}) %collective-permute-start.3) | collective-permute-done | bytes 524320 | tf_op jit(solution)/shard_map/ppermute | solution.py:20
  288.8 4.4 %fusion.43 = f32[2,2,512,256]{2,3,1,0:T(8,128)S(1)} fusion(f32[1,2,2,512,512]{4,3,2,1,0:T(8,128)} %param.14, f32[1,512,256]{1,2,0:T(8,128)} %collective-permute-done.3, f32[1,512,256]{1,2,0:T(8,128)} %collective-permute-done.2), kind=kOutput, calls=%fused_computation.43 | convolution fusion | flops 1610874880 | bytes 7340032 | tf_op jit(solution)/shard_map/fpmn,fnl->fpml/dot_general | solution.py:218
  298.8 3.8 fusion.55
  303.6 11.5 %all-to-all-start.3 = ((f32[128,2,256]{2,1,0:T(2,128)}), f32[128,2,256]{2,1,0:T(2,128)S(1)}, u32[]{:S(2)}, u32[]{:S(2)}) async-start(f32[128,2,256]{2,1,0:T(2,128)} %reshape.145), calls=%async_computation.3 | async-start | bytes 524288 | tf_op jit(solution)/shard_map/all_to_all | solution.py:223
  315.1 10.8 %all-to-all-done.3 = f32[128,2,256]{2,1,0:T(2,128)S(1)} async-done(((f32[128,2,256]{2,1,0:T(2,128)}), f32[128,2,256]{2,1,0:T(2,128)S(1)}, u32[]{:S(2)}, u32[]{:S(2)}) %all-to-all-start.3) | async-done | bytes 262176 | tf_op jit(solution)/shard_map/all_to_all | solution.py:223
  328.5 63.0 %psum.7 = f32[9,128]{1,0:T(8,128)S(1)} all-reduce(f32[9,128]{1,0:T(8,128)S(1)} %stack.47), channel_id=1, replica_groups=mesh['row'=4,'col'=32] {'row','col'}, use_global_device_ids=true, to_apply=%region_13.15 | all-reduce | flops 1152 | bytes 9216 | tf_op jit(solution)/shard_map/psum | solution.py:244
  (100 shorter events, 56.1 us)
Async XLA Ops:
  6.5 100.3 %copy-start = (f32[1,2,2,512,256]{4,3,2,1,0:T(8,128)S(1)}, f32[1,2,2,512,256]{4,3,2,1,0:T(8,128)}, u32[]{:S(2)}) copy-start(f32[1,2,2,512,256]{4,3,2,1,0:T(8,128)} %param.13) | copy-start | bytes 6291460
  6.5 52.8 %all-gather.3.cloned.1.call-start = ((), (), s32[]{:S(2)}) async-start(), calls=%async_computation.4 | async-start | bytes 4325376 | tf_op jit(solution)/shard_map/all_gather | solution.py:198
  59.4 10.7 %copy-start.3 = (f32[2,512,4096]{2,1,0:T(8,128)S(1)}, f32[2,512,4096]{2,1,0:T(8,128)}, u32[]{:S(2)}) copy-start(f32[2,512,4096]{2,1,0:T(8,128)} %param.12) | copy-start | bytes 50331652
  108.7 2.2 copy-start.1
  114.5 9.4 %collective-permute-start = (f32[1,512,256]{1,2,0:T(8,128)}, f32[1,512,256]{1,2,0:T(8,128)}, u32[]{:S(2)}, u32[]{:S(2)}) collective-permute-start(f32[1,512,256]{1,2,0:T(8,128)} %get-tuple-element.73), channel_id=1, source_target_pairs={{0,1},{1,2},{2,3},{3,4},{4,5},{5,6},{6,7},{7,8},{8,9},{9,10},{10,1... | collective-permute-start | bytes 1572872 | tf_op jit(solution)/shard_map/ppermute | solution.py:19
  117.5 10.8 %collective-permute-start.1 = (f32[1,512,256]{1,2,0:T(8,128)}, f32[1,512,256]{1,2,0:T(8,128)}, u32[]{:S(2)}, u32[]{:S(2)}) collective-permute-start(f32[1,512,256]{1,2,0:T(8,128)} %get-tuple-element.74), channel_id=1, source_target_pairs={{1,0},{2,1},{3,2},{4,3},{5,4},{6,5},{7,6},{8,7},{9,8},{10,9},{11,1... | collective-permute-start | bytes 1572872 | tf_op jit(solution)/shard_map/ppermute | solution.py:20
  133.0 5.3 %copy-start.5 = (f32[2,512,128]{2,1,0:T(8,128)S(1)}, f32[2,512,128]{2,1,0:T(8,128)}, u32[]{:S(2)}) copy-start(f32[2,512,128]{2,1,0:T(8,128)} %copy.26) | copy-start | bytes 1572868
  143.2 22.1 %all-to-all-start.1 = ((f32[128,2,256]{2,1,0:T(2,128)}), f32[128,2,256]{2,1,0:T(2,128)S(1)}, u32[]{:S(2)}, u32[]{:S(2)}) async-start(f32[128,2,256]{2,1,0:T(2,128)} %reshape.140), calls=%async_computation.1 | async-start | bytes 524288 | tf_op jit(solution)/shard_map/all_to_all | solution.py:223
  154.3 57.0 %all-gather.5.cloned.1.call-start = ((), (), s32[]{:S(2)}) async-start(), calls=%async_computation.5 | async-start | bytes 4325376 | tf_op jit(solution)/shard_map/all_gather | solution.py:198
  211.3 11.5 %copy-start.4 = (f32[4096,256]{1,0:T(8,128)S(1)}, f32[4096,256]{1,0:T(8,128)}, u32[]{:S(2)}) copy-start(f32[4096,256]{1,0:T(8,128)} %all-gather.5.cloned.1.call-done) | copy-start | bytes 12582916
  269.1 2.2 copy-start.2
  273.7 6.4 %copy-start.7 = (f32[128,256]{1,0:T(8,128)S(1)}, f32[128,256]{1,0:T(8,128)}, u32[]{:S(2)}) copy-start(f32[128,256]{1,0:T(8,128)} %param.11) | copy-start | bytes 393220
  275.0 9.4 %collective-permute-start.2 = (f32[1,512,256]{1,2,0:T(8,128)}, f32[1,512,256]{1,2,0:T(8,128)}, u32[]{:S(2)}, u32[]{:S(2)}) collective-permute-start(f32[1,512,256]{1,2,0:T(8,128)} %get-tuple-element.71), channel_id=1, source_target_pairs={{0,1},{1,2},{2,3},{3,4},{4,5},{5,6},{6,7},{7,8},{8,9},{9,10},{10,1... | collective-permute-start | bytes 1572872 | tf_op jit(solution)/shard_map/ppermute | solution.py:19
  278.0 10.8 %collective-permute-start.3 = (f32[1,512,256]{1,2,0:T(8,128)}, f32[1,512,256]{1,2,0:T(8,128)}, u32[]{:S(2)}, u32[]{:S(2)}) collective-permute-start(f32[1,512,256]{1,2,0:T(8,128)} %get-tuple-element.72), channel_id=1, source_target_pairs={{1,0},{2,1},{3,2},{4,3},{5,4},{6,5},{7,6},{8,7},{9,8},{10,9},{11,1... | collective-permute-start | bytes 1572872 | tf_op jit(solution)/shard_map/ppermute | solution.py:20
  293.4 5.3 %copy-start.6 = (f32[2,512,128]{2,1,0:T(8,128)S(1)}, f32[2,512,128]{2,1,0:T(8,128)}, u32[]{:S(2)}) copy-start(f32[2,512,128]{2,1,0:T(8,128)} %copy.37) | copy-start | bytes 1572868
  303.6 22.3 %all-to-all-start.3 = ((f32[128,2,256]{2,1,0:T(2,128)}), f32[128,2,256]{2,1,0:T(2,128)S(1)}, u32[]{:S(2)}, u32[]{:S(2)}) async-start(f32[128,2,256]{2,1,0:T(2,128)} %reshape.145), calls=%async_computation.3 | async-start | bytes 524288 | tf_op jit(solution)/shard_map/all_to_all | solution.py:223
Sparse Core Ops, SparseCore 0:
  9.6 49.7 all-gather.2
  168.5 42.7 all-gather.4
where the time goes:
time: 406 us; the launch traced here: 399 us
  waiting for transfers between devices  129 us (32%)
  blocking collectives  116 us (29%)
  matrix products  58 us (14%)
  starting transfers between devices  33 us (8%)
  local copies, waits for them, and re-layouts  30.6 us (8%)
  other arithmetic  18.5 us (5%)
  between operations  14.2 us (3%)
    all_gather x2, waiting for transfers between devices, on_device(): piece = lax.all_gather(operate_vector, 'col', axis=0, tiled=True)  93.3 us
    psum x1, blocking collectives, on_device(): sums = lax.psum(jnp.stack(sums, axis=0), ('row', 'col'))  63 us
    all_to_all x2, blocking collectives, on_device(): lax.all_to_all(buffer, ('row', 'col'), split_axis=0, concat_axis=0, tiled...  53.2 us
    all_to_all x2, starting transfers between devices, on_device(): lax.all_to_all(currents.reshape(devices, tback, lanes), ('row', 'col'), s...  22.6 us
    all_to_all x2, waiting for transfers between devices, on_device(): lax.all_to_all(currents.reshape(devices, tback, lanes), ('row', 'col'), s...  20.8 us
    dot_general x2, matrix products, on_device(): jnp.dot(real_cols, piece, precision=HIGH, preferred_element_type=jnp.floa...  19.3 us
    dot_general x2, matrix products, on_device(): jnp.dot(imag_cols, turned(piece, waves), precision=HIGH, preferred_elemen...  13.2 us
    gather x2, local copies, waits for them, and re-layouts, on_device(): jnp.take(field, trace_rows.reshape(-1), axis=0)  9.36 us
  transfers between devices with their start and end apart: 8, of which 8 were waited for; matrix products, arithmetic and copies ran while one was open for 1% of the time, Pallas kernels for 0%

commit v1 on v0

--- a/solution.py
+++ b/solution.py
@@ -2,6 +2,7 @@
 import jax.numpy as jnp
 from jax import lax
 from jax.sharding import PartitionSpec as P
+from jax.lax import all_gather
 
 ITERS = 2
 EPS = 1e-06
@@ -241,7 +242,11 @@
     u0, b0, b1 = basis
     sums = [square_terms(u0, waves), *inner_terms(u0, b0, waves), square_terms(b0, waves)]
     sums += [*inner_terms(u0, b1, waves), *inner_terms(b0, b1, waves), square_terms(b1, waves)]
-    sums = lax.psum(jnp.stack(sums, axis=0), ("row", "col"))
+
+    def plane_turn(state):
+        return all_gather(state, axis_name=("row", "col")).sum(axis=0)
+
+    sums = plane_turn(jnp.stack(sums, axis=0))
     first, second = krylov_coefficients([sums[i] for i in range(9)])
     return scale_vector(u0, first, waves) + scale_vector(b0, second, waves)
 

time: 406 us -> 378 us (0.931)
  blocking collectives: 116 us -> 88.1 us
    psum x1 -> x0, blocking collectives: 63 us -> none  [on_device(): sums = lax.psum(jnp.stack(sums, axis=0), ('row', 'col'))]
    all_gather x0 -> x1, blocking collectives: none -> 34.9 us  [plane_turn(): return all_gather(state, axis_name=('row', 'col')).sum(axis=0)]
  transfers between devices with their start and end apart: 8 -> 8, of which waited for: 8 -> 8; matrix products, arithmetic and copies ran while one was open for 1% -> 2% of each run, Pallas kernels for 0% -> 0%
where the time goes in v1:
time: 378 us; the launch traced here: 371 us
  waiting for transfers between devices  129 us (34%)
  blocking collectives  88.1 us (23%)
  matrix products  58 us (15%)
  starting transfers between devices  33 us (9%)
  local copies, waits for them, and re-layouts  30.6 us (8%)
  other arithmetic  18.7 us (5%)
  between operations  14.2 us (4%)
    all_gather x2, waiting for transfers between devices, on_device(): piece = lax.all_gather(operate_vector, 'col', axis=0, tiled=True)  93.3 us
    all_to_all x2, blocking collectives, on_device(): lax.all_to_all(buffer, ('row', 'col'), split_axis=0, concat_axis=0, tiled...  53.2 us
    all_gather x1, blocking collectives, plane_turn(): return all_gather(state, axis_name=('row', 'col')).sum(axis=0)  34.9 us
    all_to_all x2, starting transfers between devices, on_device(): lax.all_to_all(currents.reshape(devices, tback, lanes), ('row', 'col'), s...  22.6 us
    all_to_all x2, waiting for transfers between devices, on_device(): lax.all_to_all(currents.reshape(devices, tback, lanes), ('row', 'col'), s...  20.8 us
    dot_general x2, matrix products, on_device(): jnp.dot(real_cols, piece, precision=HIGH, preferred_element_type=jnp.floa...  19.3 us
    dot_general x2, matrix products, on_device(): jnp.dot(imag_cols, turned(piece, waves), precision=HIGH, preferred_elemen...  13.2 us
    gather x2, local copies, waits for them, and re-layouts, on_device(): jnp.take(field, trace_rows.reshape(-1), axis=0)  9.36 us
  transfers between devices with their start and end apart: 8, of which 8 were waited for; matrix products, arithmetic and copies ran while one was open for 2% of the time, Pallas kernels for 0%

profile of v1, /device:TPU:1, one launch (start us, length us, event | category | flops | bytes accessed | tf_op | source)
XLA Modules:
  0.0 371.5 jit_solution(12982489129436301150)
XLA Ops:
  9.0 50.4 %all-gather.5.cloned.1.call-done = f32[4096,256]{1,0:T(8,128)} async-done(((f32[128,256]{1,0:T(8,128)}), f32[4096,256]{1,0:T(8,128)}) %all-gather.5.cloned.1.call-update) | async-done | bytes 4194320 | tf_op jit(solution)/shard_map/all_gather | solution.py:199
  62.0 7.8 %fusion.6 = f32[512,256]{1,0:T(8,128)S(1)} fusion(f32[4096,256]{1,0:T(8,128)} %all-gather.5.cloned.1.call-done, f32[2,512,4096]{2,1,0:T(8,128)} %param.12), kind=kOutput, calls=%fused_computation.10 | convolution fusion | flops 3221225472 | bytes 13107200 | tf_op jit(solution)/shard_map/dot_general | solution.py:202
  70.1 3.6 fusion.63
  73.7 4.7 %gather_fusion = f32[1024,256]{1,0:T(8,128)} fusion(f32[512,256]{1,0:T(8,128)S(1)} %fusion.63, s32[1024]{0:T(1024)S(1)} %fusion.110), kind=kCustom, calls=%fused_computation.clone | custom fusion | bytes 2101248 | tf_op jit(solution)/shard_map/jit(_take)/gather | solution.py:207
  79.9 26.8 %all_to_all.20 = f32[128,8,256]{2,1,0:T(8,128)S(1)} all-to-all(f32[128,8,256]{2,1,0:T(8,128)S(1)} %bitcast_multiply_fusion.1), channel_id=1, replica_groups=mesh['row'=4,'col'=32] {'row','col'}, dimensions={0} | all-to-all | bytes 2097152 | tf_op jit(solution)/shard_map/all_to_all | solution.py:210
  114.5 3.0 collective-permute-start
  124.0 4.4 %collective-permute-done.1 = f32[1,512,256]{1,2,0:T(8,128)} collective-permute-done((f32[1,512,256]{1,2,0:T(8,128)}, f32[1,512,256]{1,2,0:T(8,128)}, u32[]{:S(2)}, u32[]{:S(2)}) %collective-permute-start.1) | collective-permute-done | bytes 524320 | tf_op jit(solution)/shard_map/ppermute | solution.py:21
  128.4 4.4 %fusion.37 = f32[2,2,512,256]{2,3,1,0:T(8,128)S(1)} fusion(f32[1,2,2,512,512]{4,3,2,1,0:T(8,128)} %param.14, f32[1,512,256]{1,2,0:T(8,128)} %collective-permute-done.1, f32[1,512,256]{1,2,0:T(8,128)} %collective-permute-done), kind=kOutput, calls=%fused_computation.41 | convolution fusion | flops 1610874880 | bytes 7340032 | tf_op jit(solution)/shard_map/fpmn,fnl->fpml/dot_general | solution.py:219
  138.3 3.8 %fusion.52 = f32[2,256,256]{1,2,0:T(8,128)S(1)} fusion(f32[1,2,256,1024]{3,2,1,0:T(8,128)} %param.15, f32[1024,128]{1,0:T(8,128)S(1)} %bitcast.201, f32[1024,128]{1,0:T(8,128)S(1)} %bitcast.199, f32[1024,128]{1,0:T(8,128)} %bitcast.205, f32[1024,128]{1,0:T(8,128)} %bitcast.203), kind=kOutput, calls=%fused_computation.46 | convolution fusion | flops 806092800 | bytes 4718592 | tf_op jit(solution)/shard_map/pkn,nl->pkl/dot_general | solution.py:222
  143.2 11.1 %all-to-all-start.1 = ((f32[128,2,256]{2,1,0:T(2,128)}), f32[128,2,256]{2,1,0:T(2,128)S(1)}, u32[]{:S(2)}, u32[]{:S(2)}) async-start(f32[128,2,256]{2,1,0:T(2,128)} %reshape.140), calls=%async_computation.1 | async-start | bytes 524288 | tf_op jit(solution)/shard_map/all_to_all | solution.py:224
  155.3 10.0 %all-to-all-done.1 = f32[128,2,256]{2,1,0:T(2,128)S(1)} async-done(((f32[128,2,256]{2,1,0:T(2,128)}), f32[128,2,256]{2,1,0:T(2,128)S(1)}, u32[]{:S(2)}, u32[]{:S(2)}) %all-to-all-start.1) | async-done | bytes 262176 | tf_op jit(solution)/shard_map/all_to_all | solution.py:224
  168.4 42.9 %all-gather.7.cloned.1.call-done = f32[4096,256]{1,0:T(8,128)} async-done(((f32[128,256]{1,0:T(8,128)}), f32[4096,256]{1,0:T(8,128)}) %all-gather.7.cloned.1.call-update) | async-done | bytes 4194320 | tf_op jit(solution)/shard_map/all_gather | solution.py:199
  211.3 11.5 %fusion.4 = f32[256,512]{1,0:T(8,128)S(1)} fusion(f32[4096,256]{1,0:T(8,128)} %all-gather.7.cloned.1.call-done, f32[2,512,4096]{2,1,0:T(8,128)} %param.12), kind=kOutput, calls=%fused_computation.8 | convolution fusion | flops 3221225472 | bytes 13107200 | tf_op jit(solution)/shard_map/dot_general | solution.py:202
  223.1 9.6 %fusion.73 = f32[512,256]{0,1:T(8,128)S(1)} fusion(f32[256,512]{1,0:T(8,128)S(1)} %fusion.4, f32[2,512,4096]{2,1,0:T(8,128)} %param.12, f32[4096,128]{1,0:T(8,128)S(1)} %get-tuple-element.44, f32[4096,128]{1,0:T(8,128)S(1)} %get-tuple-element.43), kind=kOutput, calls=%fused_computation.51 | convolution fusion | flops 3222405120 | bytes 13631488 | tf_op jit(solution)/shard_map/dot_general | solution.py:203
  232.8 4.7 %gather_fusion.1 = f32[1024,256]{1,0:T(8,128)} fusion(f32[512,256]{1,0:T(8,128)S(1)} %copy.57, s32[1024]{0:T(1024)S(1)} %fusion.110), kind=kCustom, calls=%fused_computation.1.clone | custom fusion | bytes 2101248 | tf_op jit(solution)/shard_map/jit(_take)/gather | solution.py:207
  239.1 26.5 %all_to_all.21 = f32[128,8,256]{2,1,0:T(8,128)S(1)} all-to-all(f32[128,8,256]{2,1,0:T(8,128)S(1)} %bitcast_multiply_fusion), channel_id=1, replica_groups=mesh['row'=4,'col'=32] {'row','col'}, dimensions={0} | all-to-all | bytes 2097152 | tf_op jit(solution)/shard_map/all_to_all | solution.py:210
  275.0 3.0 collective-permute-start.2
  281.4 3.1 collective-permute-done.2
  284.4 4.4 %collective-permute-done.3 = f32[1,512,256]{1,2,0:T(8,128)} collective-permute-done((f32[1,512,256]{1,2,0:T(8,128)}, f32[1,512,256]{1,2,0:T(8,128)}, u32[]{:S(2)}, u32[]{:S(2)}) %collective-permute-start.3) | collective-permute-done | bytes 524320 | tf_op jit(solution)/shard_map/ppermute | solution.py:21
  288.8 4.4 %fusion.43 = f32[2,2,512,256]{2,3,1,0:T(8,128)S(1)} fusion(f32[1,2,2,512,512]{4,3,2,1,0:T(8,128)} %param.14, f32[1,512,256]{1,2,0:T(8,128)} %collective-permute-done.3, f32[1,512,256]{1,2,0:T(8,128)} %collective-permute-done.2), kind=kOutput, calls=%fused_computation.43 | convolution fusion | flops 1610874880 | bytes 7340032 | tf_op jit(solution)/shard_map/fpmn,fnl->fpml/dot_general | solution.py:219
  298.8 3.8 %fusion.55 = f32[2,256,256]{1,2,0:T(8,128)S(1)} fusion(f32[1,2,256,1024]{3,2,1,0:T(8,128)} %param.15, f32[1024,128]{1,0:T(8,128)S(1)} %bitcast.202, f32[1024,128]{1,0:T(8,128)S(1)} %bitcast.200, f32[1024,128]{1,0:T(8,128)} %bitcast.206, f32[1024,128]{1,0:T(8,128)} %bitcast.204), kind=kOutput, calls=%fused_computation.47 | convolution fusion | flops 806092800 | bytes 4718592 | tf_op jit(solution)/shard_map/pkn,nl->pkl/dot_general | solution.py:222
  303.6 11.5 %all-to-all-start.3 = ((f32[128,2,256]{2,1,0:T(2,128)}), f32[128,2,256]{2,1,0:T(2,128)S(1)}, u32[]{:S(2)}, u32[]{:S(2)}) async-start(f32[128,2,256]{2,1,0:T(2,128)} %reshape.145), calls=%async_computation.3 | async-start | bytes 524288 | tf_op jit(solution)/shard_map/all_to_all | solution.py:224
  315.1 10.8 %all-to-all-done.3 = f32[128,2,256]{2,1,0:T(2,128)S(1)} async-done(((f32[128,2,256]{2,1,0:T(2,128)}), f32[128,2,256]{2,1,0:T(2,128)S(1)}, u32[]{:S(2)}, u32[]{:S(2)}) %all-to-all-start.3) | async-done | bytes 262176 | tf_op jit(solution)/shard_map/all_to_all | solution.py:224
  328.5 34.9 %all-gather.1 = f32[128,9,128]{2,1,0:T(8,128)S(1)} all-gather(f32[1,9,128]{2,1,0:T(8,128)S(1)} %bitcast.207), channel_id=2, replica_groups=mesh['row'=4,'col'=32] {'row','col'}, dimensions={0}, use_global_device_ids=true | all-gather | bytes 594432 | tf_op jit(solution)/shard_map/all_gather | solution.py:247
  (101 shorter events, 56.3 us)
Async XLA Ops:
  6.5 100.3 %copy-start = (f32[1,2,2,512,256]{4,3,2,1,0:T(8,128)S(1)}, f32[1,2,2,512,256]{4,3,2,1,0:T(8,128)}, u32[]{:S(2)}) copy-start(f32[1,2,2,512,256]{4,3,2,1,0:T(8,128)} %param.13) | copy-start | bytes 6291460
  6.5 52.8 %all-gather.5.cloned.1.call-start = ((), (), s32[]{:S(2)}) async-start(), calls=%async_computation.4 | async-start | bytes 4325376 | tf_op jit(solution)/shard_map/all_gather | solution.py:199
  59.4 10.7 %copy-start.3 = (f32[2,512,4096]{2,1,0:T(8,128)S(1)}, f32[2,512,4096]{2,1,0:T(8,128)}, u32[]{:S(2)}) copy-start(f32[2,512,4096]{2,1,0:T(8,128)} %param.12) | copy-start | bytes 50331652
  108.7 2.2 copy-start.1
  114.5 9.4 %collective-permute-start = (f32[1,512,256]{1,2,0:T(8,128)}, f32[1,512,256]{1,2,0:T(8,128)}, u32[]{:S(2)}, u32[]{:S(2)}) collective-permute-start(f32[1,512,256]{1,2,0:T(8,128)} %get-tuple-element.73), channel_id=1, source_target_pairs={{0,1},{1,2},{2,3},{3,4},{4,5},{5,6},{6,7},{7,8},{8,9},{9,10},{10,1... | collective-permute-start | bytes 1572872 | tf_op jit(solution)/shard_map/ppermute | solution.py:20
  117.5 10.8 %collective-permute-start.1 = (f32[1,512,256]{1,2,0:T(8,128)}, f32[1,512,256]{1,2,0:T(8,128)}, u32[]{:S(2)}, u32[]{:S(2)}) collective-permute-start(f32[1,512,256]{1,2,0:T(8,128)} %get-tuple-element.74), channel_id=1, source_target_pairs={{1,0},{2,1},{3,2},{4,3},{5,4},{6,5},{7,6},{8,7},{9,8},{10,9},{11,1... | collective-permute-start | bytes 1572872 | tf_op jit(solution)/shard_map/ppermute | solution.py:21
  133.0 5.3 %copy-start.5 = (f32[2,512,128]{2,1,0:T(8,128)S(1)}, f32[2,512,128]{2,1,0:T(8,128)}, u32[]{:S(2)}) copy-start(f32[2,512,128]{2,1,0:T(8,128)} %copy.50) | copy-start | bytes 1572868
  143.2 22.1 %all-to-all-start.1 = ((f32[128,2,256]{2,1,0:T(2,128)}), f32[128,2,256]{2,1,0:T(2,128)S(1)}, u32[]{:S(2)}, u32[]{:S(2)}) async-start(f32[128,2,256]{2,1,0:T(2,128)} %reshape.140), calls=%async_computation.1 | async-start | bytes 524288 | tf_op jit(solution)/shard_map/all_to_all | solution.py:224
  154.3 57.0 %all-gather.7.cloned.1.call-start = ((), (), s32[]{:S(2)}) async-start(), calls=%async_computation.5 | async-start | bytes 4325376 | tf_op jit(solution)/shard_map/all_gather | solution.py:199
  211.3 11.5 %copy-start.4 = (f32[4096,256]{1,0:T(8,128)S(1)}, f32[4096,256]{1,0:T(8,128)}, u32[]{:S(2)}) copy-start(f32[4096,256]{1,0:T(8,128)} %all-gather.7.cloned.1.call-done) | copy-start | bytes 12582916
  269.1 2.2 copy-start.2
  273.7 6.4 %copy-start.7 = (f32[128,256]{1,0:T(8,128)S(1)}, f32[128,256]{1,0:T(8,128)}, u32[]{:S(2)}) copy-start(f32[128,256]{1,0:T(8,128)} %param.11) | copy-start | bytes 393220
  275.0 9.4 %collective-permute-start.2 = (f32[1,512,256]{1,2,0:T(8,128)}, f32[1,512,256]{1,2,0:T(8,128)}, u32[]{:S(2)}, u32[]{:S(2)}) collective-permute-start(f32[1,512,256]{1,2,0:T(8,128)} %get-tuple-element.71), channel_id=1, source_target_pairs={{0,1},{1,2},{2,3},{3,4},{4,5},{5,6},{6,7},{7,8},{8,9},{9,10},{10,1... | collective-permute-start | bytes 1572872 | tf_op jit(solution)/shard_map/ppermute | solution.py:20
  278.0 10.8 %collective-permute-start.3 = (f32[1,512,256]{1,2,0:T(8,128)}, f32[1,512,256]{1,2,0:T(8,128)}, u32[]{:S(2)}, u32[]{:S(2)}) collective-permute-start(f32[1,512,256]{1,2,0:T(8,128)} %get-tuple-element.72), channel_id=1, source_target_pairs={{1,0},{2,1},{3,2},{4,3},{5,4},{6,5},{7,6},{8,7},{9,8},{10,9},{11,1... | collective-permute-start | bytes 1572872 | tf_op jit(solution)/shard_map/ppermute | solution.py:21
  293.4 5.3 %copy-start.6 = (f32[2,512,128]{2,1,0:T(8,128)S(1)}, f32[2,512,128]{2,1,0:T(8,128)}, u32[]{:S(2)}) copy-start(f32[2,512,128]{2,1,0:T(8,128)} %copy.61) | copy-start | bytes 1572868
  303.6 22.3 %all-to-all-start.3 = ((f32[128,2,256]{2,1,0:T(2,128)}), f32[128,2,256]{2,1,0:T(2,128)S(1)}, u32[]{:S(2)}, u32[]{:S(2)}) async-start(f32[128,2,256]{2,1,0:T(2,128)} %reshape.145), calls=%async_computation.3 | async-start | bytes 524288 | tf_op jit(solution)/shard_map/all_to_all | solution.py:224
Sparse Core Ops, SparseCore 0:
  9.6 49.7 all-gather.4
  168.5 42.7 all-gather.6
